TPU v7x, 512 devices: a whole 4x4x16 slice. The times are simulated.
512 devices in a mesh: seq: 64 (over z, y), head: 8 (over x, core).
Axes of the slice: x: 4, y: 4, z: 16, core: 2. Of those that a mesh axis runs over, the one named last changes fastest.
Arguments:
- queries: bfloat16 [8192, 8192], P('seq', 'head'), may hold values from -6 to 6
- keys: bfloat16 [8192, 8192], P('seq', 'head'), may hold values from -6 to 6
- values: bfloat16 [8192, 8192], P('seq', 'head'), may hold values from -140 to 140
- log_decay: float32 [8192, 64], P('seq', 'head'), may hold values from -1.5 to 0, as said below
- gain: float32 [8192], P('head'), may hold values from 0.25 to 1.75
- cotangent: bfloat16 [8192, 8192], P('seq', 'head'), may hold values from -6 to 6
Outputs:
- normed: bfloat16 [8192, 8192], P('seq', 'head')
- grad_queries: bfloat16 [8192, 8192], P('seq', 'head')
- grad_keys: bfloat16 [8192, 8192], P('seq', 'head')
- grad_values: bfloat16 [8192, 8192], P('seq', 'head')
Inputs may be any that keep to these rules, and one draw needn't show every extreme that they name: `log_decay`: negative everywhere.
All inputs are finite; a program needn't handle non-finite values.
Results may differ from a plain program's by a relative error of at most 0.007.
Values sent between devices are 32-bit elements; how exact they have to be, the bound alone decides.
A program may use at most 128 MiB of HBM per device.

v0:
```python
import jax
import jax.numpy as jnp
from jax import lax
from jax.sharding import PartitionSpec as P

EPSILON = 1e-05


def carried_in(part, axis, combine, identity, reverse):
    count = lax.axis_size(axis)
    place = lax.axis_index(axis)
    ahead = count - 1 - place if reverse else place
    gathered = jax.tree.map(lambda a: lax.all_gather(a, axis), part)
    state = jax.tree.map(lambda a, e: jnp.zeros_like(a) + jnp.asarray(e, a.dtype), part, identity)

    def one(turn, state):
        source = count - 1 - turn if reverse else turn
        return combine(
            state, jax.tree.map(lambda a: lax.dynamic_index_in_dim(a, source, 0, False), gathered)
        )

    return lax.fori_loop(0, ahead, one, state)


def chain_combine(earlier, later):
    return (earlier[0] + later[0], jnp.exp(later[0])[:, None, None] * earlier[1] + later[1])


def per_device(queries, keys, values, log_decay, gain, cotangent):
    tokens, row_width = queries.shape
    head_count = log_decay.shape[1]
    head_size = row_width // head_count
    scaling = head_size ** (-0.5)
    features = row_width * lax.axis_size("head")
    shape = (tokens, head_count, head_size)
    query_rows = queries.reshape(shape)
    key_rows = keys.reshape(shape)
    value_rows = values.reshape(shape)
    gain_rows = gain.reshape(head_count, head_size)
    cumulative = jnp.cumsum(log_decay, axis=0)
    block_total = cumulative[-1]
    by_head = cumulative.T
    gaps = by_head[:, :, None] - by_head[:, None, :]
    causal = (
        lax.broadcasted_iota(jnp.int32, (tokens, tokens), 0)
        >= lax.broadcasted_iota(jnp.int32, (tokens, tokens), 1)
    )[None]
    weights = jnp.where(causal, jnp.exp(jnp.where(causal, gaps, 0.0)), 0.0) * scaling
    tail = jnp.exp(block_total[None, :] - cumulative)
    keys_decayed = (key_rows * tail[:, :, None]).astype(jnp.bfloat16)
    block_state = jnp.einsum(
        "jhd,jhe->hde", keys_decayed, value_rows, preferred_element_type=jnp.float32
    )
    zero_state = (
        jnp.zeros((head_count,), jnp.float32),
        jnp.zeros((head_count, head_size, head_size), jnp.float32),
    )
    incoming = carried_in((block_total, block_state), "seq", chain_combine, zero_state, False)[
        1
    ].astype(jnp.bfloat16)
    scores = (
        jnp.einsum("thd,jhd->htj", query_rows, key_rows, preferred_element_type=jnp.float32)
        * weights
    ).astype(jnp.bfloat16)
    row_scale = scaling * jnp.exp(cumulative)
    queried = (query_rows * row_scale[:, :, None]).astype(jnp.bfloat16)
    attended = jnp.einsum("htj,jhd->thd", scores, value_rows, preferred_element_type=jnp.float32)
    attended = attended + jnp.einsum(
        "thd,hde->the", queried, incoming, preferred_element_type=jnp.float32
    )
    upstream = cotangent.reshape(shape) * gain_rows
    square_part = jnp.sum(attended * attended, axis=(1, 2))
    square_sum = lax.psum(square_part, "head")
    inverse = lax.rsqrt(square_sum / features + EPSILON)
    unit_rows = attended * inverse[:, None, None]
    slope_unit = lax.psum(jnp.sum(upstream * unit_rows, axis=(1, 2)), "head")
    grad_out = (
        inverse[:, None, None] * upstream
        - unit_rows * (inverse * slope_unit / features)[:, None, None]
    )
    normed = (
        (attended * inverse[:, None, None] * gain_rows)
        .astype(jnp.bfloat16)
        .reshape(tokens, row_width)
    )
    grad_out = grad_out.astype(jnp.bfloat16)
    grad_state = jnp.einsum("thd,the->hde", queried, grad_out, preferred_element_type=jnp.float32)
    outgoing = carried_in((block_total, grad_state), "seq", chain_combine, zero_state, True)[
        1
    ].astype(jnp.bfloat16)
    grad_scores = (
        jnp.einsum("the,jhe->htj", grad_out, value_rows, preferred_element_type=jnp.float32)
        * weights
    ).astype(jnp.bfloat16)
    grad_query = jnp.einsum(
        "htj,jhd->thd", grad_scores, key_rows, preferred_element_type=jnp.float32
    )
    grad_query = (
        grad_query
        + jnp.einsum("the,hde->thd", grad_out, incoming, preferred_element_type=jnp.float32)
        * row_scale[:, :, None]
    )
    grad_key = jnp.einsum(
        "htj,thd->jhd", grad_scores, query_rows, preferred_element_type=jnp.float32
    )
    grad_key = (
        grad_key
        + jnp.einsum("jhe,hde->jhd", value_rows, outgoing, preferred_element_type=jnp.float32)
        * tail[:, :, None]
    )
    grad_value = jnp.einsum("htj,the->jhe", scores, grad_out, preferred_element_type=jnp.float32)
    grad_value = grad_value + jnp.einsum(
        "jhd,hde->jhe", keys_decayed, outgoing, preferred_element_type=jnp.float32
    )
    flat = (tokens, row_width)
    return (
        normed,
        grad_query.astype(jnp.bfloat16).reshape(flat),
        grad_key.astype(jnp.bfloat16).reshape(flat),
        grad_value.astype(jnp.bfloat16).reshape(flat),
    )


def solution(mesh):
    placed = (
        P("seq", "head"),
        P("seq", "head"),
        P("seq", "head"),
        P("seq", "head"),
        P("head"),
        P("seq", "head"),
    )
    return jax.shard_map(
        per_device,
        mesh=mesh,
        in_specs=placed,
        out_specs=(P("seq", "head"), P("seq", "head"), P("seq", "head"), P("seq", "head")),
        check_vma=False,
    )
```

profile of v0, /device:TPU:1, one launch (start us, length us, event | category | flops | bytes accessed | tf_op | source)
XLA Modules:
  0.0 783.8 jit_solution(8477541993744561257)
XLA Ops:
  12.9 72.7 %all-gather.2 = f32[64,1,8]{2,1,0:T(1,128)S(1)} all-gather(f32[1,1,8]{2,1,0:T(1,128)S(1)} %get-tuple-element.167), channel_id=1, replica_groups=mesh['seq'=64,'head'=8] {'seq'}, dimensions={0}, use_global_device_ids=true | all-gather | bytes 2080 | tf_op jit(solution)/shard_map/all_gather | solution.py:13
  86.0 222.5 %all-gather.6.cloned.1.call-done = f32[512,128,128]{2,1,0:T(8,128)} async-done(((f32[8,128,128]{2,1,0:T(8,128)}), f32[512,128,128]{2,1,0:T(8,128)}) %all-gather.6.cloned.1.call-update) | async-done | bytes 33554448 | tf_op jit(solution)/shard_map/all_gather | solution.py:13
  309.2 13.2 %psum.14 = f32[128]{0:T(128)S(1)} all-reduce(f32[128]{0:T(128)S(1)} %get-tuple-element.168), channel_id=1, replica_groups=mesh['seq'=64,'head'=8] {'head'}, use_global_device_ids=true, to_apply=%region_4.5 | all-reduce | flops 128 | bytes 1024 | tf_op jit(solution)/shard_map/psum | solution.py:73
  323.3 13.8 %psum.15 = f32[128]{0:T(128)S(1)} all-reduce(f32[128]{0:T(128)S(1)} %multiply_reduce_fusion), channel_id=1, replica_groups=mesh['seq'=64,'head'=8] {'head'}, use_global_device_ids=true, to_apply=%region_6.7 | all-reduce | flops 128 | bytes 1024 | tf_op jit(solution)/shard_map/psum | solution.py:76
  342.2 354.5 %all-gather.8.cloned.1.call-done = f32[512,128,128]{2,1,0:T(8,128)} async-done(((f32[8,128,128]{2,1,0:T(8,128)}), f32[512,128,128]{2,1,0:T(8,128)}) %all-gather.8.cloned.1.call-update) | async-done | bytes 33554448 | tf_op jit(solution)/shard_map/all_gather | solution.py:13
  696.7 77.9 %while.27 = (s32[]{:T(128)}, f32[8,128,128]{2,1,0:T(8,128)S(1)}, s32[]{:T(128)}, f32[64,8]{1,0:T(8,128)S(1)}, f32[64,8,128,128]{3,2,1,0:T(8,128)}, /*index=5*/s32[]{:T(128)}, s32[]{:T(128)}, s32[]{:T(128)}, s32[]{:T(128)}) while((s32[]{:T(128)}, f32[8,128,128]{2,1,0:T(8,128)S(1)}, s32[]{:T(128)}, f32[64,8]{1,0:T(8,128)S(1)}, ...), condition=%wide.region_8.9_spmd, body=%wide.region_7.8_spmd.sunk | while | flops 262150 | bytes 1573115 | solution.py:22
  696.8 1.2 bitcast_add_fusion.5
  699.3 1.2 bitcast_add_fusion.5
  701.7 1.2 bitcast_add_fusion.5
  703.0 1.2 bitcast_add_fusion.5
  704.2 1.2 bitcast_add_fusion.5
  705.4 1.2 bitcast_add_fusion.5
  706.7 1.2 bitcast_add_fusion.5
  707.9 1.2 bitcast_add_fusion.5
  710.4 1.2 bitcast_add_fusion.5
  712.9 1.2 bitcast_add_fusion.5
  715.3 1.2 bitcast_add_fusion.5
  717.8 1.2 bitcast_add_fusion.5
  720.3 1.2 bitcast_add_fusion.5
  722.7 1.2 bitcast_add_fusion.5
  725.2 1.2 bitcast_add_fusion.5
  726.4 1.2 bitcast_add_fusion.5
  727.7 1.2 bitcast_add_fusion.5
  728.9 1.2 bitcast_add_fusion.5
  (148 shorter events, 69.4 us)
Async XLA Ops:
  7.2 2.3 copy-start
  7.2 301.3 %all-gather.6.cloned.1.call-start = ((), (), s32[]{:S(2)}) async-start(), calls=%async_computation | async-start | bytes 34078720 | tf_op jit(solution)/shard_map/all_gather | solution.py:13
  10.5 686.2 %all-gather.8.cloned.1.call-start = ((), (), s32[]{:S(2)}) async-start(), calls=%async_computation.1 | async-start | bytes 34078720 | tf_op jit(solution)/shard_map/all_gather | solution.py:13
Sparse Core Ops, SparseCore 0:
  10.9 297.5 all-gather.5
  339.3 357.3 all-gather.7
where the time goes:
time: 787 us; the launch traced here: 784 us
  waiting for transfers between devices  577 us (73%)
  blocking collectives  99.7 us (13%)
  other arithmetic  77.1 us (10%)
  between operations  14.2 us (2%)
  local copies, waits for them, and re-layouts  8.73 us (1%)
    all_gather x2, waiting for transfers between devices, carried_in(): gathered = jax.tree.map(lambda a: lax.all_gather(a, axis), part)  577 us
    add x63, other arithmetic, chain_combine(): jnp.exp(later[0])[:, None, None] * earlier[1] + later[1]  75 us
    all_gather x1, blocking collectives, carried_in(): gathered = jax.tree.map(lambda a: lax.all_gather(a, axis), part)  72.7 us
  transfers between devices with their start and end apart: 2, of which 2 were waited for; matrix products, arithmetic and copies ran while one was open for 1% of the time, Pallas kernels for 0%

commit v1 on v0

--- a/solution.py
+++ b/solution.py
@@ -6,24 +6,22 @@
 EPSILON = 1e-05
 
 
-def carried_in(part, axis, combine, identity, reverse):
+def carried_in(part, axis, reverse):
+    total, state = part
     count = lax.axis_size(axis)
     place = lax.axis_index(axis)
-    ahead = count - 1 - place if reverse else place
-    gathered = jax.tree.map(lambda a: lax.all_gather(a, axis), part)
-    state = jax.tree.map(lambda a, e: jnp.zeros_like(a) + jnp.asarray(e, a.dtype), part, identity)
-
-    def one(turn, state):
-        source = count - 1 - turn if reverse else turn
-        return combine(
-            state, jax.tree.map(lambda a: lax.dynamic_index_in_dim(a, source, 0, False), gathered)
-        )
-
-    return lax.fori_loop(0, ahead, one, state)
-
-
-def chain_combine(earlier, later):
-    return (earlier[0] + later[0], jnp.exp(later[0])[:, None, None] * earlier[1] + later[1])
+    heads = total.shape[0]
+    totals = lax.all_gather(total, axis)
+    mine = lax.dynamic_index_in_dim(totals, place * heads // count, 1, False)
+    at = jnp.arange(count)
+    first, last = (at[:, None], at[None, :]) if reverse else (at[None, :], at[:, None])
+    between = (at > first[:, :, None]) & (at < last[:, :, None])
+    gaps = jnp.sum(jnp.where(between, mine, 0.0), axis=-1)
+    decay = jnp.where(first < last, 0.5 * jnp.exp(gaps), 0.0)
+    pieces = state.reshape(count, -1, state.shape[-1])
+    swapped = lax.all_to_all(pieces, axis, 0, 0, tiled=True)
+    summed = jnp.einsum("ab,bcd->acd", decay, swapped, precision=lax.Precision.HIGHEST)
+    return 2.0 * lax.all_to_all(summed, axis, 0, 0, tiled=True).reshape(state.shape)
 
 
 def per_device(queries, keys, values, log_decay, gain, cotangent):
@@ -51,13 +49,7 @@
     block_state = jnp.einsum(
         "jhd,jhe->hde", keys_decayed, value_rows, preferred_element_type=jnp.float32
     )
-    zero_state = (
-        jnp.zeros((head_count,), jnp.float32),
-        jnp.zeros((head_count, head_size, head_size), jnp.float32),
-    )
-    incoming = carried_in((block_total, block_state), "seq", chain_combine, zero_state, False)[
-        1
-    ].astype(jnp.bfloat16)
+    incoming = carried_in((block_total, block_state), "seq", False).astype(jnp.bfloat16)
     scores = (
         jnp.einsum("thd,jhd->htj", query_rows, key_rows, preferred_element_type=jnp.float32)
         * weights
@@ -85,9 +77,7 @@
     )
     grad_out = grad_out.astype(jnp.bfloat16)
     grad_state = jnp.einsum("thd,the->hde", queried, grad_out, preferred_element_type=jnp.float32)
-    outgoing = carried_in((block_total, grad_state), "seq", chain_combine, zero_state, True)[
-        1
-    ].astype(jnp.bfloat16)
+    outgoing = carried_in((block_total, grad_state), "seq", True).astype(jnp.bfloat16)
     grad_scores = (
         jnp.einsum("the,jhe->htj", grad_out, value_rows, preferred_element_type=jnp.float32)
         * weights

time: 787 us -> 259 us (0.33)
  the two profiles are of different devices: /device:TPU:1 before, /device:TPU:8 now
where the time goes in v1:
time: 259 us; the launch traced here: 258 us
  blocking collectives  157 us (61%)
  waiting for transfers between devices  50.3 us (19%)
  starting transfers between devices  34.4 us (13%)
  local copies, waits for them, and re-layouts  8.72 us (3%)
  matrix products  5.58 us (2%)
    all_gather x1, blocking collectives, carried_in(): totals = lax.all_gather(total, axis)  93.3 us
    all_to_all x2, waiting for transfers between devices, carried_in(): lax.all_to_all(summed, axis, 0, 0, tiled=True).reshape(state.shape)  50.3 us
    all_to_all x1, blocking collectives, carried_in(): swapped = lax.all_to_all(pieces, axis, 0, 0, tiled=True)  38.5 us
    all_to_all x1, starting transfers between devices, carried_in(): swapped = lax.all_to_all(pieces, axis, 0, 0, tiled=True)  18.7 us
    all_to_all x2, starting transfers between devices, carried_in(): lax.all_to_all(summed, axis, 0, 0, tiled=True).reshape(state.shape)  15.6 us
    psum x1, blocking collectives, per_device(): slope_unit = lax.psum(jnp.sum(upstream * unit_rows, axis=(1, 2)), 'head')  12.4 us
    psum x1, blocking collectives, per_device(): square_sum = lax.psum(square_part, 'head')  12.4 us
    unnamed x18, local copies, waits for them, and re-layouts  5.31 us
  transfers between devices with their start and end apart: 3, of which 2 were waited for; matrix products, arithmetic and copies ran while one was open for 2% of the time, Pallas kernels for 0%

profile of v1, /device:TPU:8, one launch (start us, length us, event | category | flops | bytes accessed | tf_op | source)
XLA Modules:
  0.0 258.4 jit_solution(9052369710395033278)
XLA Ops:
  0.7 0.8 copy.99
  2.0 1.0 fusion.17
  3.0 18.7 %all-to-all-start = ((f32[64,16,128]{2,1,0:T(8,128)}), f32[64,16,128]{2,1,0:T(8,128)S(1)}, u32[]{:S(2)}, u32[]{:S(2)}) async-start(f32[64,16,128]{2,1,0:T(8,128)} %bitcast.7), calls=%async_computation | async-start | bytes 1048576 | tf_op jit(solution)/shard_map/all_to_all | solution.py:22
  21.7 93.3 %all-gather = f32[64,1,8]{2,1,0:T(1,128)S(1)} all-gather(f32[1,1,8]{2,1,0:T(1,128)S(1)} %get-tuple-element.26), channel_id=1, replica_groups=mesh['seq'=64,'head'=8] {'seq'}, dimensions={0}, use_global_device_ids=true | all-gather | bytes 2080 | tf_op jit(solution)/shard_map/all_gather | solution.py:14
  115.0 0.9 dynamic-slice_reduce_fusion
  116.0 1.2 select_reduce_fusion
  117.1 0.7 fusion.12
  117.9 1.1 copy.106
  119.0 9.7 %all-to-all-start.1 = ((f32[64,16,128]{2,1,0:T(8,128)}), f32[64,16,128]{2,1,0:T(8,128)S(1)}, u32[]{:S(2)}, u32[]{:S(2)}) async-start(f32[64,16,128]{2,1,0:T(8,128)} %copy.106), calls=%async_computation.1 | async-start | bytes 1048576 | tf_op jit(solution)/shard_map/all_to_all | solution.py:24
  129.0 0.6 copy-done.1
  130.1 21.4 %all-to-all-done.1 = f32[64,16,128]{2,1,0:T(8,128)S(1)} async-done(((f32[64,16,128]{2,1,0:T(8,128)}), f32[64,16,128]{2,1,0:T(8,128)S(1)}, u32[]{:S(2)}, u32[]{:S(2)}) %all-to-all-start.1) | async-done | bytes 524320 | tf_op jit(solution)/shard_map/all_to_all | solution.py:24
  151.9 0.4 multiply_reduce_fusion.1
  152.3 12.4 %psum.14 = f32[128]{0:T(128)S(1)} all-reduce(f32[128]{0:T(128)S(1)} %get-tuple-element.28), channel_id=1, replica_groups=mesh['seq'=64,'head'=8] {'head'}, use_global_device_ids=true, to_apply=%region_3.4 | all-reduce | flops 128 | bytes 1024 | tf_op jit(solution)/shard_map/psum | solution.py:65
  164.9 12.4 %psum.15 = f32[128]{0:T(128)S(1)} all-reduce(f32[128]{0:T(128)S(1)} %multiply_reduce_fusion), channel_id=1, replica_groups=mesh['seq'=64,'head'=8] {'head'}, use_global_device_ids=true, to_apply=%region_5.6 | all-reduce | flops 128 | bytes 1024 | tf_op jit(solution)/shard_map/psum | solution.py:68
  177.9 38.5 %all_to_all.20 = f32[64,16,128]{2,1,0:T(8,128)S(1)} all-to-all(f32[64,16,128]{2,1,0:T(8,128)S(1)} %bitcast.105), channel_id=1, replica_groups=mesh['seq'=64,'head'=8] {'seq'}, dimensions={0} | all-to-all | bytes 1048576 | tf_op jit(solution)/shard_map/all_to_all | solution.py:22
  216.4 0.7 fusion.10
  217.1 1.1 copy.116
  218.2 6.0 %all-to-all-start.3 = ((f32[64,16,128]{2,1,0:T(8,128)}), f32[64,16,128]{2,1,0:T(8,128)S(1)}, u32[]{:S(2)}, u32[]{:S(2)}) async-start(f32[64,16,128]{2,1,0:T(8,128)} %copy.116), calls=%async_computation.3 | async-start | bytes 1048576 | tf_op jit(solution)/shard_map/all_to_all | solution.py:24
  224.1 0.3 fusion.7
  225.0 0.9 copy.121
  225.9 0.8 copy.120
  227.2 28.9 %all-to-all-done.3 = f32[64,16,128]{2,1,0:T(8,128)S(1)} async-done(((f32[64,16,128]{2,1,0:T(8,128)}), f32[64,16,128]{2,1,0:T(8,128)S(1)}, u32[]{:S(2)}, u32[]{:S(2)}) %all-to-all-start.3) | async-done | bytes 524320 | tf_op jit(solution)/shard_map/all_to_all | solution.py:24
  256.4 0.9 copy.123
  257.6 0.9 copy.122
  (36 shorter events, 3.9 us)
Async XLA Ops:
  0.6 1.3 copy-start
  0.6 1.1 copy-start.2
  3.0 114.2 %all-to-all-start = ((f32[64,16,128]{2,1,0:T(8,128)}), f32[64,16,128]{2,1,0:T(8,128)S(1)}, u32[]{:S(2)}, u32[]{:S(2)}) async-start(f32[64,16,128]{2,1,0:T(8,128)} %bitcast.7), calls=%async_computation | async-start | bytes 1048576 | tf_op jit(solution)/shard_map/all_to_all | solution.py:22
  119.0 9.8 %copy-start.3 = (bf16[128,1024]{1,0:T(8,128)(2,1)S(1)}, bf16[128,1024]{1,0:T(8,128)(2,1)}, u32[]{:S(2)}) copy-start(bf16[128,1024]{1,0:T(8,128)(2,1)} %param.6) | copy-start | bytes 786436
  119.0 32.6 %all-to-all-start.1 = ((f32[64,16,128]{2,1,0:T(8,128)}), f32[64,16,128]{2,1,0:T(8,128)S(1)}, u32[]{:S(2)}, u32[]{:S(2)}) async-start(f32[64,16,128]{2,1,0:T(8,128)} %copy.106), calls=%async_computation.1 | async-start | bytes 1048576 | tf_op jit(solution)/shard_map/all_to_all | solution.py:24
  128.7 1.0 copy-start.1
  151.9 12.8 %copy-start.4 = (f32[1024]{0:T(1024)S(1)}, f32[1024]{0:T(1024)}, u32[]{:S(2)}) copy-start(f32[1024]{0:T(1024)} %param.10) | copy-start | bytes 12292
  218.2 37.9 %all-to-all-start.3 = ((f32[64,16,128]{2,1,0:T(8,128)}), f32[64,16,128]{2,1,0:T(8,128)S(1)}, u32[]{:S(2)}, u32[]{:S(2)}) async-start(f32[64,16,128]{2,1,0:T(8,128)} %copy.116), calls=%async_computation.3 | async-start | bytes 1048576 | tf_op jit(solution)/shard_map/all_to_all | solution.py:24

commit v2 on v1

v2 whole, which is shorter than its diff:
```python
import functools

import jax
import jax.numpy as jnp
from jax import lax
from jax.experimental import pallas as pl
from jax.experimental.pallas import tpu as pltpu
from jax.sharding import PartitionSpec as P

EPSILON = 1e-05
SIDE = 4
F32 = jnp.float32
BF16 = jnp.bfloat16
HIGHEST = lax.Precision.HIGHEST


def dot(a, b, contract, precision=None):
    return lax.dot_general(
        a, b, ((contract[:1], contract[1:]), ((), ())), precision=precision,
        preferred_element_type=F32,
    )


def exchange_order(count):
    return sorted(range(1, count), key=lambda d: -min(d, count - d))


class Exchange:
    def __init__(self, source, target, send_sem, recv_sem, place, count, device, shared=False):
        self.source, self.target, self.place, self.count = source, target, place, count
        self.send_sem, self.recv_sem, self.device, self.shared = send_sem, recv_sem, device, shared
        self.started = []

    def copy(self, peer, slot, step):
        return pltpu.make_async_remote_copy(
            src_ref=self.source if self.shared else self.source.at[peer],
            dst_ref=self.target.at[slot],
            send_sem=self.send_sem.at[step],
            recv_sem=self.recv_sem.at[step],
            device_id=self.device(peer),
            device_id_type=pl.DeviceIdType.MESH,
        )

    def start(self):
        for step in exchange_order(self.count):
            copy = self.copy(lax.rem(self.place + step, self.count), self.place, step)
            copy.start()
            self.started.append(copy)
        self.target[self.place] = self.source[...] if self.shared else self.source[self.place]

    def finish(self):
        for step in range(1, self.count):
            peer = lax.rem(self.place + self.count - step, self.count)
            self.copy(peer, peer, step).wait_recv()

    def drain(self):
        for copy in self.started:
            copy.wait_send()


def kernel(
    seq_count, group, features,
    q_ref, k_ref, v_ref, ld_ref, gain_ref, cot_ref,
    normed_ref, gq_ref, gk_ref, gv_ref,
    w_ref, sc_ref, ds_ref, o_ref, u_ref, gkl_ref, gvl_ref, qd_ref, kd_ref, do_ref, s_ref,
    yb, yrb, zb, zrb, zo, zi, yo, yi,
    yb2, yrb2, zb2, zrb2, zo2, zi2, yo2, yi2,
    hs, hr,
    ys, yr, zs, zr, hs_sem, hr_sem,
):
    tokens = q_ref.shape[0]
    heads = ld_ref.shape[1]
    size = q_ref.shape[1] // heads
    depth = seq_count // SIDE
    own = heads // SIDE
    span = own * size // depth
    scaling = size ** (-0.5)
    seq, head = lax.axis_index("seq"), lax.axis_index("head")
    z, y = seq // SIDE, lax.rem(seq, SIDE)
    def y_peer(p):
        return (z * SIDE + p, head)

    def z_peer(p):
        return (p * SIDE + y, head)

    def h_peer(p):
        return (seq, p)

    barrier = pltpu.get_barrier_semaphore()
    for place, count, device in ((y, SIDE, y_peer), (z, depth, z_peer), (head, group, h_peer)):
        for step in range(1, count):
            pl.semaphore_signal(
                barrier, inc=1, device_id=device(lax.rem(place + step, count)),
                device_id_type=pl.DeviceIdType.MESH,
            )

    def at(h):
        return slice(h * size, (h + 1) * size)

    row = lax.broadcasted_iota(jnp.int32, (tokens, tokens), 0)
    column = lax.broadcasted_iota(jnp.int32, (tokens, tokens), 1)
    causal = row >= column
    lower = jnp.where(causal, 1.0, 0.0).astype(F32)
    log_decay = ld_ref[...]
    c = dot(lower, log_decay, (1, 0), HIGHEST)
    c_rows = dot(log_decay, lower, (0, 1), HIGHEST)
    total = jnp.broadcast_to(c_rows[:, tokens - 1:tokens], (heads, size))
    tail = jnp.exp(c[tokens - 1:tokens, :] - c)
    row_scale = scaling * jnp.exp(c)

    for h in range(heads):
        kd = (k_ref[:, at(h)].astype(F32) * tail[:, h:h + 1]).astype(BF16)
        kd_ref[:, at(h)] = kd
        place = h % own
        yb[h // own, at(place)] = dot(kd, v_ref[:, at(h)], (0, 0))
        yb[h // own, own * size + place * 8:own * size + place * 8 + 8] = jnp.broadcast_to(
            total[h:h + 1], (8, size)
        )
    pl.semaphore_wait(barrier, SIDE + depth + group - 3)

    exchanges = []

    def exchange(source, target, index, sems, place, count, device, shared=False):
        made = Exchange(
            source, target, sems[0].at[index], sems[1].at[index], place, count, device, shared
        )
        made.start()
        exchanges.append(made)
        return made

    def own_total(part, place):
        first = own * size + place * 8
        return yrb[part, first:first + 1]

    def own_decay(part, place):
        return jnp.exp(own_total(part, place))

    moving = exchange(yb, yrb, 0, (ys, yr), y, SIDE, y_peer)
    for h in range(heads):
        gaps = c[:, h:h + 1] - c_rows[h:h + 1, :]
        weights = jnp.where(causal, jnp.exp(jnp.where(causal, gaps, 0.0)), 0.0) * scaling
        w_ref[h] = weights
        sc_ref[h] = (dot(q_ref[:, at(h)], k_ref[:, at(h)], (1, 1)) * weights).astype(BF16)
    moving.finish()
    for place in range(own):
        state = yrb[0, at(place)]
        whole = own_total(0, place)
        for part in range(1, SIDE):
            state = own_decay(part, place) * state + yrb[part, at(place)]
            whole = whole + own_total(part, place)
        slots = slice(place * size // span, (place + 1) * size // span)
        zb[slots, 0:span] = state.reshape(size // span, span, size)
        zb[slots, span:span + 8] = jnp.broadcast_to(whole, (size // span, 8, size))
    moving = exchange(zb, zrb, 0, (zs, zr), z, depth, z_peer)
    for h in range(heads):
        o_ref[:, at(h)] = dot(sc_ref[h], v_ref[:, at(h)], (1, 0))
    moving.finish()
    state = jnp.zeros((span, size), F32)
    for part in range(depth):
        zo[part] = state
        state = jnp.exp(zrb[part, span:span + 1]) * state + zrb[part, 0:span]
    moving = exchange(zo, zi, 1, (zs, zr), z, depth, z_peer)
    for h in range(heads):
        qd_ref[:, at(h)] = (q_ref[:, at(h)].astype(F32) * row_scale[:, h:h + 1]).astype(BF16)
        u_ref[:, at(h)] = cot_ref[:, at(h)].astype(F32) * gain_ref[:, at(h)]
    moving.finish()
    for place in range(own):
        slots = slice(place * size // span, (place + 1) * size // span)
        state = zi[slots].reshape(size, size)
        for part in range(SIDE):
            yo[part, at(place)] = state
            if part < SIDE - 1:
                state = own_decay(part, place) * state + yrb[part, at(place)]
    moving = exchange(yo, yi, 1, (ys, yr), y, SIDE, y_peer)
    moving.finish()

    squares = jnp.zeros((tokens, size), F32)
    slopes = jnp.zeros((tokens, size), F32)
    for h in range(heads):
        state = yi[h // own, at(h % own)].astype(BF16)
        s_ref[h] = state
        o = o_ref[:, at(h)] + dot(qd_ref[:, at(h)], state, (1, 0))
        o_ref[:, at(h)] = o
        squares = squares + o * o
        slopes = slopes + u_ref[:, at(h)] * o
    hs[0:8] = jnp.broadcast_to(jnp.sum(jnp.transpose(squares), axis=0, keepdims=True), (8, tokens))
    hs[8:16] = jnp.broadcast_to(jnp.sum(jnp.transpose(slopes), axis=0, keepdims=True), (8, tokens))
    moving = exchange(hs, hr, 0, (hs_sem, hr_sem), head, group, h_peer, True)
    moving.finish()
    both = hr[0]
    for part in range(1, group):
        both = both + hr[part]
    inverse_row = lax.rsqrt(both[0:1] / features + EPSILON)
    pull_row = inverse_row * inverse_row * (inverse_row * both[8:9]) / features
    inverse = jnp.transpose(jnp.broadcast_to(inverse_row, (size, tokens)))
    pull = jnp.transpose(jnp.broadcast_to(pull_row, (size, tokens)))

    for h in range(heads):
        do = (inverse * u_ref[:, at(h)] - o_ref[:, at(h)] * pull).astype(BF16)
        do_ref[:, at(h)] = do
        yb2[h // own, at(h % own)] = dot(qd_ref[:, at(h)], do, (0, 0))
    moving = exchange(yb2, yrb2, 2, (ys, yr), y, SIDE, y_peer)
    for h in range(heads):
        normed_ref[:, at(h)] = (o_ref[:, at(h)] * inverse * gain_ref[:, at(h)]).astype(BF16)
        ds_ref[h] = (dot(do_ref[:, at(h)], v_ref[:, at(h)], (1, 1)) * w_ref[h]).astype(BF16)
    moving.finish()
    for place in range(own):
        state = yrb2[SIDE - 1, at(place)]
        for part in reversed(range(SIDE - 1)):
            state = own_decay(part, place) * state + yrb2[part, at(place)]
        slots = slice(place * size // span, (place + 1) * size // span)
        zb2[slots] = state.reshape(size // span, span, size)
    moving = exchange(zb2, zrb2, 2, (zs, zr), z, depth, z_peer)
    for h in range(heads):
        gq_ref[:, at(h)] = (
            dot(ds_ref[h], k_ref[:, at(h)], (1, 0))
            + dot(do_ref[:, at(h)], s_ref[h], (1, 1)) * row_scale[:, h:h + 1]
        ).astype(BF16)
    moving.finish()
    state = jnp.zeros((span, size), F32)
    for part in reversed(range(depth)):
        zo2[part] = state
        state = jnp.exp(zrb[part, span:span + 1]) * state + zrb2[part]
    moving = exchange(zo2, zi2, 3, (zs, zr), z, depth, z_peer)
    for h in range(heads):
        gkl_ref[:, at(h)] = dot(ds_ref[h], q_ref[:, at(h)], (0, 0))
        gvl_ref[:, at(h)] = dot(sc_ref[h], do_ref[:, at(h)], (0, 0))
    moving.finish()
    for place in range(own):
        slots = slice(place * size // span, (place + 1) * size // span)
        state = zi2[slots].reshape(size, size)
        for part in reversed(range(SIDE)):
            yo2[part, at(place)] = state
            if part > 0:
                state = own_decay(part, place) * state + yrb2[part, at(place)]
    moving = exchange(yo2, yi2, 3, (ys, yr), y, SIDE, y_peer)
    moving.finish()
    for h in range(heads):
        state = yi2[h // own, at(h % own)].astype(BF16)
        gk_ref[:, at(h)] = (
            gkl_ref[:, at(h)] + dot(v_ref[:, at(h)], state, (1, 1)) * tail[:, h:h + 1]
        ).astype(BF16)
        gv_ref[:, at(h)] = (gvl_ref[:, at(h)] + dot(kd_ref[:, at(h)], state, (1, 0))).astype(BF16)
    for made in exchanges:
        made.drain()


def per_device(queries, keys, values, log_decay, gain, cotangent):
    tokens, width = queries.shape
    heads = log_decay.shape[1]
    size = width // heads
    seq_count, group = lax.axis_size("seq"), lax.axis_size("head")
    depth = seq_count // SIDE
    own = heads // SIDE
    span = own * size // depth
    block = pl.BlockSpec(memory_space=pltpu.VMEM)
    square = (heads, tokens, tokens)
    flat = (tokens, width)
    V = pltpu.VMEM
    with_totals = [
        V((SIDE, own * (size + 8), size), F32), V((SIDE, own * (size + 8), size), F32),
        V((depth, span + 8, size), F32), V((depth, span + 8, size), F32),
    ]
    y_slots, z_slots = V((SIDE, own * size, size), F32), V((depth, span, size), F32)
    back = [z_slots, z_slots, y_slots, y_slots]
    out = jax.ShapeDtypeStruct(flat, BF16)
    return pl.pallas_call(
        functools.partial(kernel, seq_count, group, float(width * group)),
        out_shape=(out, out, out, out),
        in_specs=[block] * 6,
        out_specs=(block,) * 4,
        scratch_shapes=[
            V(square, F32), V(square, BF16), V(square, BF16),
            V(flat, F32), V(flat, F32), V(flat, F32), V(flat, F32),
            V(flat, BF16), V(flat, BF16), V(flat, BF16),
            V((heads, size, size), BF16),
            *with_totals, *back,
            y_slots, y_slots, z_slots, z_slots, *back,
            V((16, tokens), F32), V((group, 16, tokens), F32),
            pltpu.SemaphoreType.DMA((4, SIDE)), pltpu.SemaphoreType.DMA((4, SIDE)),
            pltpu.SemaphoreType.DMA((4, depth)), pltpu.SemaphoreType.DMA((4, depth)),
            pltpu.SemaphoreType.DMA((1, group)), pltpu.SemaphoreType.DMA((1, group)),
        ],
        compiler_params=pltpu.CompilerParams(collective_id=0, has_side_effects=True),
        name="attention_both_ways",
    )(queries, keys, values, log_decay, gain.reshape(1, width), cotangent)


def solution(mesh):
    placed = (
        P("seq", "head"),
        P("seq", "head"),
        P("seq", "head"),
        P("seq", "head"),
        P("head"),
        P("seq", "head"),
    )
    return jax.shard_map(
        per_device,
        mesh=mesh,
        in_specs=placed,
        out_specs=(P("seq", "head"), P("seq", "head"), P("seq", "head"), P("seq", "head")),
        check_vma=False,
    )
```

time: 259 us -> 95.1 us (0.37)
  blocking collectives: 157 us -> 0 us
  Pallas kernels: 0 us -> 88.2 us
  waiting for transfers between devices: 50.3 us -> 0 us
  starting transfers between devices: 34.4 us -> 0 us
  matrix products: 5.58 us -> 0 us
  local copies, waits for them, and re-layouts: 8.72 us -> 5.92 us
    all_gather x1 -> x0, blocking collectives: 93.3 us -> none  [carried_in(): totals = lax.all_gather(total, axis)]
    pallas_call x0 -> x1, Pallas kernels: none -> 88.2 us  [per_device(): pl.pallas_call(functools.partial(kernel, seq_count, group, float(width *...]
    all_to_all x3 -> x0, waiting for transfers between devices: 50.3 us -> none  [the longest x2 50.3 us: carried_in(): lax.all_to_all(summed, axis, 0, 0, tiled=True).reshape(state.shape)]
    all_to_all x1 -> x0, blocking collectives: 38.5 us -> none  [carried_in(): swapped = lax.all_to_all(pieces, axis, 0, 0, tiled=True)]
    all_to_all x3 -> x0, starting transfers between devices: 34.4 us -> none  [the longest x1 18.7 us: carried_in(): swapped = lax.all_to_all(pieces, axis, 0, 0, tiled=True)]
    psum x2 -> x0, blocking collectives: 24.8 us -> none  [the longest x1 12.4 us: per_device(): slope_unit = lax.psum(jnp.sum(upstream * unit_rows, axis=(1, 2)), 'head')]
    dot_general x14 -> x0, matrix products: 5.58 us -> none  [the longest x2 1.44 us: carried_in(): jnp.einsum('ab,bcd->acd', decay, swapped, precision=lax.Precision.HIGHEST)]
    unnamed x18 -> x11, local copies, waits for them, and re-layouts: 5.31 us -> 5.92 us
  transfers between devices with their start and end apart: 3 -> 0, of which waited for: 2 -> 0; matrix products, arithmetic and copies ran while one was open for 2% -> 0% of each run, Pallas kernels for 0% -> 0%
where the time goes in v2:
time: 95.1 us; the launch traced here: 94.8 us
  Pallas kernels  88.2 us (93%)
  local copies, waits for them, and re-layouts  5.92 us (6%)
    pallas_call x1, Pallas kernels, per_device(): pl.pallas_call(functools.partial(kernel, seq_count, group, float(width *...  88.2 us
    unnamed x11, local copies, waits for them, and re-layouts  5.92 us

profile of v2, /device:TPU:8, one launch (start us, length us, event | category | flops | bytes accessed | tf_op | source)
XLA Modules:
  0.0 94.8 jit_solution(15303087524016500829)
XLA Ops:
  0.6 1.4 %copy.10.ld_ref = f32[128,8]{1,0:T(8,128)} copy(f32[128,8]{0,1:T(8,128)} %param.9) | data formatting | bytes 8192 | tf_op args[3]
  2.0 88.2 %attention_both_ways.1 = (bf16[128,1024]{1,0:T(8,128)(2,1)}, bf16[128,1024]{1,0:T(8,128)(2,1)}, bf16[128,1024]{1,0:T(8,128)(2,1)}, bf16[128,1024]{1,0:T(8,128)(2,1)}) custom-call(bf16[128,1024]{1,0:T(8,128)(2,1)} %q_ref.1, bf16[128,1024]{1,0:T(8,128)(2,1)} %k_ref.1, bf16[128,1024]{1,0:T(8,128)(2,1)} %v_ref.1, f32[128,8]{1,0:T(8,128)} %copy.10.ld_ref, ...), custom_call_target="tpu_custom_call" | custom-call | tf_op jit(solution)/shard_map/attention_both_ways/pallas_call | solution.py:267
  90.3 0.0 copy-start.2
  90.3 1.7 %copy.15 = bf16[128,1024]{1,0:T(8,128)(2,1)} copy(bf16[128,1024]{1,0:T(8,128)(2,1)} %get-tuple-element.8) | data formatting | bytes 524288
  92.0 0.0 copy-done.2
  92.0 0.0 copy-start.1
  92.0 0.7 copy.16
  92.7 0.3 copy-done.1
  93.1 0.0 copy-start
  93.1 0.7 copy.17
  93.8 0.3 copy-done
  94.1 0.7 copy.18
Async XLA Ops:
  90.3 1.7 %copy-start.2 = (bf16[128,1024]{1,0:T(8,128)(2,1)S(1)}, bf16[128,1024]{1,0:T(8,128)(2,1)}, u32[]{:S(2)}) copy-start(bf16[128,1024]{1,0:T(8,128)(2,1)} %get-tuple-element.9) | copy-start | bytes 786436
  92.0 1.0 %copy-start.1 = (bf16[128,1024]{1,0:T(8,128)(2,1)S(1)}, bf16[128,1024]{1,0:T(8,128)(2,1)}, u32[]{:S(2)}) copy-start(bf16[128,1024]{1,0:T(8,128)(2,1)} %get-tuple-element.10) | copy-start | bytes 786436
  93.1 1.0 %copy-start = (bf16[128,1024]{1,0:T(8,128)(2,1)S(1)}, bf16[128,1024]{1,0:T(8,128)(2,1)}, u32[]{:S(2)}) copy-start(bf16[128,1024]{1,0:T(8,128)(2,1)} %get-tuple-element.11) | copy-start | bytes 786436

commit v3 on v2

v3 whole, which is shorter than its diff:
```python
import functools

import jax
import jax.numpy as jnp
from jax import lax
from jax.experimental import pallas as pl
from jax.experimental.pallas import tpu as pltpu
from jax.sharding import PartitionSpec as P

EPSILON = 1e-05
SIDE = 4
F32 = jnp.float32
BF16 = jnp.bfloat16
HIGHEST = lax.Precision.HIGHEST


def dot(a, b, contract, precision=None):
    return lax.dot_general(
        a, b, ((contract[:1], contract[1:]), ((), ())), precision=precision,
        preferred_element_type=F32,
    )


def exchange_order(count):
    return sorted(range(1, count), key=lambda d: -min(d, count - d))


class Exchange:
    def __init__(self, source, target, send_sem, recv_sem, place, count, device, shared=False):
        self.source, self.target, self.place, self.count = source, target, place, count
        self.send_sem, self.recv_sem, self.device, self.shared = send_sem, recv_sem, device, shared
        self.started = []

    def copy(self, peer, slot, step):
        return pltpu.make_async_remote_copy(
            src_ref=self.source if self.shared else self.source.at[peer],
            dst_ref=self.target.at[slot],
            send_sem=self.send_sem.at[step],
            recv_sem=self.recv_sem.at[step],
            device_id=self.device(peer),
            device_id_type=pl.DeviceIdType.MESH,
        )

    def start(self):
        for step in exchange_order(self.count):
            copy = self.copy(lax.rem(self.place + step, self.count), self.place, step)
            copy.start()
            self.started.append(copy)
        self.target[self.place] = self.source[...] if self.shared else self.source[self.place]

    def finish(self):
        for step in range(1, self.count):
            peer = lax.rem(self.place + self.count - step, self.count)
            self.copy(peer, peer, step).wait_recv()

    def drain(self):
        for copy in self.started:
            copy.wait_send()


def kernel(
    seq_count, group, features,
    q_ref, k_ref, v_ref, ld_ref, gain_ref, cot_ref,
    normed_ref, gq_ref, gk_ref, gv_ref,
    w_ref, sc_ref, ds_ref, o_ref, u_ref, gkl_ref, gvl_ref, qd_ref, kd_ref, do_ref, s_ref,
    yb, yrb, zb, zrb, zo, zi, yo, yi,
    yb2, yrb2, zb2, zrb2, zo2, zi2, yo2, yi2,
    tb, trb, tz, tzr, hs, hr,
    ys, yr, zs, zr, hs_sem, hr_sem,
):
    tokens = q_ref.shape[0]
    heads = ld_ref.shape[0]
    size = q_ref.shape[1] // heads
    depth = seq_count // SIDE
    own = heads // SIDE
    span = size // depth
    scaling = size ** (-0.5)
    seq, head = lax.axis_index("seq"), lax.axis_index("head")
    z, y = seq // SIDE, lax.rem(seq, SIDE)

    def y_peer(p):
        return (z * SIDE + p, head)

    def z_peer(p):
        return (p * SIDE + y, head)

    def h_peer(p):
        return (seq, p)

    barrier = pltpu.get_barrier_semaphore()
    for place, count, device in ((z, depth, z_peer), (y, SIDE, y_peer), (head, group, h_peer)):
        for step in exchange_order(count):
            pl.semaphore_signal(
                barrier, inc=1, device_id=device(lax.rem(place + step, count)),
                device_id_type=pl.DeviceIdType.MESH,
            )

    exchanges = []

    def exchange(source, target, sems, index, place, count, device, shared=False):
        made = Exchange(
            source, target, sems[0].at[index], sems[1].at[index], place, count, device, shared
        )
        made.start()
        exchanges.append(made)
        return made

    def over_y(source, target, index, shared=False):
        return exchange(source, target, (ys, yr), index, y, SIDE, y_peer, shared)

    def over_z(source, target, index, shared=False):
        return exchange(source, target, (zs, zr), index, z, depth, z_peer, shared)

    def at(h):
        return slice(h * size, (h + 1) * size)

    units = range(own)
    in_order = [part * own + unit for unit in units for part in range(SIDE)]
    row = lax.broadcasted_iota(jnp.int32, (tokens, tokens), 0)
    column = lax.broadcasted_iota(jnp.int32, (tokens, tokens), 1)
    causal = row >= column
    lower = jnp.where(causal, 1.0, 0.0).astype(F32)
    log_decay = ld_ref[...]
    c = dot(lower, log_decay, (1, 1), HIGHEST)
    c_rows = dot(log_decay, lower, (1, 1), HIGHEST)
    total = jnp.broadcast_to(c_rows[:, tokens - 1:tokens], (heads, size))
    for part in range(SIDE):
        tb[part] = total[part * own:(part + 1) * own]
    tail = jnp.exp(c[tokens - 1:tokens, :] - c)
    row_scale = scaling * jnp.exp(c)

    for h in in_order:
        kd = (k_ref[:, at(h)].astype(F32) * tail[:, h:h + 1]).astype(BF16)
        kd_ref[:, at(h)] = kd
        yb[h % own, h // own] = dot(kd, v_ref[:, at(h)], (0, 0))
    pl.semaphore_wait(barrier, SIDE + depth + group - 3)

    totals = over_y(tb, trb, 0)
    moving = [over_y(yb.at[unit], yrb.at[unit], 1 + unit) for unit in units]
    totals.finish()
    whole = trb[0]
    for part in range(1, SIDE):
        whole = whole + trb[part]
    tz[...] = whole
    wholes = over_z(tz, tzr, 0, True)

    def own_decay(part, unit):
        return jnp.exp(trb[part, unit:unit + 1])

    for h in in_order:
        gaps = c[:, h:h + 1] - c_rows[h:h + 1, :]
        weights = jnp.where(causal, jnp.exp(jnp.where(causal, gaps, 0.0)), 0.0) * scaling
        w_ref[h] = weights
        sc_ref[h] = (dot(q_ref[:, at(h)], k_ref[:, at(h)], (1, 1)) * weights).astype(BF16)
    out = []
    for unit in units:
        moving[unit].finish()
        state = yrb[unit, 0]
        for part in range(1, SIDE):
            state = own_decay(part, unit) * state + yrb[unit, part]
        zb[unit] = state.reshape(depth, span, size)
        out.append(over_z(zb.at[unit], zrb.at[unit], 1 + unit))
    for h in in_order:
        o_ref[:, at(h)] = dot(sc_ref[h], v_ref[:, at(h)], (1, 0))
    wholes.finish()
    moving = []
    for unit in units:
        out[unit].finish()
        state = jnp.zeros((span, size), F32)
        for part in range(depth):
            zo[unit, part] = state
            state = jnp.exp(tzr[part, unit:unit + 1]) * state + zrb[unit, part]
        moving.append(over_z(zo.at[unit], zi.at[unit], 1 + own + unit))
    for h in in_order:
        qd_ref[:, at(h)] = (q_ref[:, at(h)].astype(F32) * row_scale[:, h:h + 1]).astype(BF16)
        u_ref[:, at(h)] = cot_ref[:, at(h)].astype(F32) * gain_ref[:, at(h)]
    out = []
    for unit in units:
        moving[unit].finish()
        state = zi[unit].reshape(size, size)
        for part in range(SIDE):
            yo[unit, part] = state
            if part < SIDE - 1:
                state = own_decay(part, unit) * state + yrb[unit, part]
        out.append(over_y(yo.at[unit], yi.at[unit], 1 + own + unit))

    squares = jnp.zeros((tokens, size), F32)
    slopes = jnp.zeros((tokens, size), F32)
    for unit in units:
        out[unit].finish()
        for part in range(SIDE):
            h = part * own + unit
            state = yi[unit, part].astype(BF16)
            s_ref[h] = state
            o = o_ref[:, at(h)] + dot(qd_ref[:, at(h)], state, (1, 0))
            o_ref[:, at(h)] = o
            squares = squares + o * o
            slopes = slopes + u_ref[:, at(h)] * o
    hs[0:1] = jnp.sum(jnp.transpose(squares), axis=0, keepdims=True)
    hs[1:2] = jnp.sum(jnp.transpose(slopes), axis=0, keepdims=True)
    exchange(hs, hr, (hs_sem, hr_sem), 0, head, group, h_peer, True).finish()
    both = hr[0]
    for part in range(1, group):
        both = both + hr[part]
    inverse_row = lax.rsqrt(both[0:1] / features + EPSILON)
    pull_row = inverse_row * inverse_row * (inverse_row * both[1:2]) / features
    inverse = jnp.transpose(jnp.broadcast_to(inverse_row, (size, tokens)))
    pull = jnp.transpose(jnp.broadcast_to(pull_row, (size, tokens)))

    first = 1 + 2 * own
    moving = []
    for unit in units:
        for part in range(SIDE):
            h = part * own + unit
            do = (inverse * u_ref[:, at(h)] - o_ref[:, at(h)] * pull).astype(BF16)
            do_ref[:, at(h)] = do
            yb2[unit, part] = dot(qd_ref[:, at(h)], do, (0, 0))
        moving.append(over_y(yb2.at[unit], yrb2.at[unit], first + unit))
    for h in in_order:
        ds_ref[h] = (dot(do_ref[:, at(h)], v_ref[:, at(h)], (1, 1)) * w_ref[h]).astype(BF16)
    out = []
    for unit in units:
        moving[unit].finish()
        state = yrb2[unit, SIDE - 1]
        for part in reversed(range(SIDE - 1)):
            state = own_decay(part, unit) * state + yrb2[unit, part]
        zb2[unit] = state.reshape(depth, span, size)
        out.append(over_z(zb2.at[unit], zrb2.at[unit], first + unit))
    for h in in_order:
        normed_ref[:, at(h)] = (o_ref[:, at(h)] * inverse * gain_ref[:, at(h)]).astype(BF16)
        gq_ref[:, at(h)] = (
            dot(ds_ref[h], k_ref[:, at(h)], (1, 0))
            + dot(do_ref[:, at(h)], s_ref[h], (1, 1)) * row_scale[:, h:h + 1]
        ).astype(BF16)
    moving = []
    for unit in units:
        out[unit].finish()
        state = jnp.zeros((span, size), F32)
        for part in reversed(range(depth)):
            zo2[unit, part] = state
            state = jnp.exp(tzr[part, unit:unit + 1]) * state + zrb2[unit, part]
        moving.append(over_z(zo2.at[unit], zi2.at[unit], first + own + unit))
    for h in in_order:
        gkl_ref[:, at(h)] = dot(ds_ref[h], q_ref[:, at(h)], (0, 0))
        gvl_ref[:, at(h)] = dot(sc_ref[h], do_ref[:, at(h)], (0, 0))
    out = []
    for unit in units:
        moving[unit].finish()
        state = zi2[unit].reshape(size, size)
        for part in reversed(range(SIDE)):
            yo2[unit, part] = state
            if part > 0:
                state = own_decay(part, unit) * state + yrb2[unit, part]
        out.append(over_y(yo2.at[unit], yi2.at[unit], first + own + unit))
    for unit in units:
        out[unit].finish()
        for part in range(SIDE):
            h = part * own + unit
            state = yi2[unit, part].astype(BF16)
            gk_ref[:, at(h)] = (
                gkl_ref[:, at(h)] + dot(v_ref[:, at(h)], state, (1, 1)) * tail[:, h:h + 1]
            ).astype(BF16)
            gv_ref[:, at(h)] = (
                gvl_ref[:, at(h)] + dot(kd_ref[:, at(h)], state, (1, 0))
            ).astype(BF16)
    for made in exchanges:
        made.drain()


def per_device(queries, keys, values, log_decay, gain, cotangent):
    tokens, width = queries.shape
    heads = log_decay.shape[1]
    size = width // heads
    seq_count, group = lax.axis_size("seq"), lax.axis_size("head")
    depth = seq_count // SIDE
    own = heads // SIDE
    block = pl.BlockSpec(memory_space=pltpu.VMEM)
    square = (heads, tokens, tokens)
    flat = (tokens, width)
    V = pltpu.VMEM
    Sem = pltpu.SemaphoreType.DMA
    y_slots = V((own, SIDE, size, size), F32)
    z_slots = V((own, depth, size // depth, size), F32)
    way = [y_slots, y_slots, z_slots, z_slots, z_slots, z_slots, y_slots, y_slots]
    steps = 1 + 4 * own
    out = jax.ShapeDtypeStruct(flat, BF16)
    return pl.pallas_call(
        functools.partial(kernel, seq_count, group, float(width * group)),
        out_shape=(out, out, out, out),
        in_specs=[block] * 6,
        out_specs=(block,) * 4,
        scratch_shapes=[
            V(square, F32), V(square, BF16), V(square, BF16),
            V(flat, F32), V(flat, F32), V(flat, F32), V(flat, F32),
            V(flat, BF16), V(flat, BF16), V(flat, BF16),
            V((heads, size, size), BF16),
            *way, *way,
            V((SIDE, own, size), F32), V((SIDE, own, size), F32),
            V((own, size), F32), V((depth, own, size), F32),
            V((2, tokens), F32), V((group, 2, tokens), F32),
            Sem((steps, SIDE)), Sem((steps, SIDE)),
            Sem((steps, depth)), Sem((steps, depth)),
            Sem((1, group)), Sem((1, group)),
        ],
        compiler_params=pltpu.CompilerParams(collective_id=0, has_side_effects=True),
        name="attention_both_ways",
    )(queries, keys, values, log_decay.T, gain.reshape(1, width), cotangent)


def solution(mesh):
    placed = (
        P("seq", "head"),
        P("seq", "head"),
        P("seq", "head"),
        P("seq", "head"),
        P("head"),
        P("seq", "head"),
    )
    return jax.shard_map(
        per_device,
        mesh=mesh,
        in_specs=placed,
        out_specs=(P("seq", "head"), P("seq", "head"), P("seq", "head"), P("seq", "head")),
        check_vma=False,
    )
```

time: 95.1 us -> 86.6 us (0.911)
  the two profiles are of different devices: /device:TPU:8 before, /device:TPU:32 now
where the time goes in v3:
time: 86.6 us; the launch traced here: 86.4 us
  Pallas kernels  81.2 us (94%)
  local copies, waits for them, and re-layouts  4.5 us (5%)
    pallas_call x1, Pallas kernels, per_device(): pl.pallas_call(functools.partial(kernel, seq_count, group, float(width *...  81.2 us
    unnamed x10, local copies, waits for them, and re-layouts  4.5 us

profile of v3, /device:TPU:32, one launch (start us, length us, event | category | flops | bytes accessed | tf_op | source)
XLA Modules:
  0.0 86.4 jit_solution(4364742149092520358)
XLA Ops:
  0.6 81.2 %attention_both_ways.1 = (bf16[128,1024]{1,0:T(8,128)(2,1)}, bf16[128,1024]{1,0:T(8,128)(2,1)}, bf16[128,1024]{1,0:T(8,128)(2,1)}, bf16[128,1024]{1,0:T(8,128)(2,1)}) custom-call(bf16[128,1024]{1,0:T(8,128)(2,1)} %q_ref.1, bf16[128,1024]{1,0:T(8,128)(2,1)} %k_ref.1, bf16[128,1024]{1,0:T(8,128)(2,1)} %v_ref.1, f32[8,128]{1,0:T(8,128)} %bitcast.2, ...), custom_call_target="tpu_custom_call" | custom-call | tf_op jit(solution)/shard_map/attention_both_ways/pallas_call | solution.py:287
  81.9 0.0 copy-start.2
  81.9 1.7 %copy.14 = bf16[128,1024]{1,0:T(8,128)(2,1)} copy(bf16[128,1024]{1,0:T(8,128)(2,1)} %get-tuple-element.8) | data formatting | bytes 524288
  83.6 0.0 copy-done.2
  83.6 0.0 copy-start.1
  83.6 0.7 copy.15
  84.3 0.3 copy-done.1
  84.6 0.0 copy-start
  84.6 0.7 copy.16
  85.3 0.3 copy-done
  85.7 0.7 copy.17
Async XLA Ops:
  81.9 1.7 %copy-start.2 = (bf16[128,1024]{1,0:T(8,128)(2,1)S(1)}, bf16[128,1024]{1,0:T(8,128)(2,1)}, u32[]{:S(2)}) copy-start(bf16[128,1024]{1,0:T(8,128)(2,1)} %get-tuple-element.9) | copy-start | bytes 786436
  83.6 1.0 %copy-start.1 = (bf16[128,1024]{1,0:T(8,128)(2,1)S(1)}, bf16[128,1024]{1,0:T(8,128)(2,1)}, u32[]{:S(2)}) copy-start(bf16[128,1024]{1,0:T(8,128)(2,1)} %get-tuple-element.10) | copy-start | bytes 786436
  84.6 1.0 %copy-start = (bf16[128,1024]{1,0:T(8,128)(2,1)S(1)}, bf16[128,1024]{1,0:T(8,128)(2,1)}, u32[]{:S(2)}) copy-start(bf16[128,1024]{1,0:T(8,128)(2,1)} %get-tuple-element.11) | copy-start | bytes 786436

commit v4 on v3

--- a/solution.py
+++ b/solution.py
@@ -9,6 +9,7 @@
 
 EPSILON = 1e-05
 SIDE = 4
+CUT = 1
 F32 = jnp.float32
 BF16 = jnp.bfloat16
 HIGHEST = lax.Precision.HIGHEST
@@ -60,20 +61,29 @@
 
 def kernel(
     seq_count, group, features,
-    q_ref, k_ref, v_ref, ld_ref, gain_ref, cot_ref,
+    q_in, k_in, v_in, ld_in, gain_in, cot_in,
     normed_ref, gq_ref, gk_ref, gv_ref,
     w_ref, sc_ref, ds_ref, o_ref, u_ref, gkl_ref, gvl_ref, qd_ref, kd_ref, do_ref, s_ref,
     yb, yrb, zb, zrb, zo, zi, yo, yi,
     yb2, yrb2, zb2, zrb2, zo2, zi2, yo2, yi2,
     tb, trb, tz, tzr, hs, hr,
     ys, yr, zs, zr, hs_sem, hr_sem,
+    q_ref, k_ref, v_ref, ld_ref, gain_ref, cot_ref, in_sem,
 ):
+    loads = [
+        pltpu.make_async_copy(source, target, in_sem.at[i])
+        for i, (source, target) in enumerate((
+            (ld_in, ld_ref), (k_in, k_ref), (v_in, v_ref),
+            (q_in, q_ref), (cot_in, cot_ref), (gain_in, gain_ref),
+        ))
+    ]
     tokens = q_ref.shape[0]
     heads = ld_ref.shape[0]
     size = q_ref.shape[1] // heads
     depth = seq_count // SIDE
     own = heads // SIDE
-    span = size // depth
+    rows = size // CUT
+    span = rows // depth
     scaling = size ** (-0.5)
     seq, head = lax.axis_index("seq"), lax.axis_index("head")
     z, y = seq // SIDE, lax.rem(seq, SIDE)
@@ -95,6 +105,8 @@
                 device_id_type=pl.DeviceIdType.MESH,
             )
 
+    for load in loads:
+        load.start()
     exchanges = []
 
     def exchange(source, target, sems, index, place, count, device, shared=False):
@@ -114,12 +126,18 @@
     def at(h):
         return slice(h * size, (h + 1) * size)
 
-    units = range(own)
-    in_order = [part * own + unit for unit in units for part in range(SIDE)]
+    units = range(own * CUT)
+    in_order = [part * own + place for place in range(own) for part in range(SIDE)]
+
+    def put(slots, h, value):
+        for piece in range(CUT):
+            slots[h % own * CUT + piece, h // own] = value[piece * rows:(piece + 1) * rows]
+
     row = lax.broadcasted_iota(jnp.int32, (tokens, tokens), 0)
     column = lax.broadcasted_iota(jnp.int32, (tokens, tokens), 1)
     causal = row >= column
     lower = jnp.where(causal, 1.0, 0.0).astype(F32)
+    loads[0].wait()
     log_decay = ld_ref[...]
     c = dot(lower, log_decay, (1, 1), HIGHEST)
     c_rows = dot(log_decay, lower, (1, 1), HIGHEST)
@@ -129,10 +147,14 @@
     tail = jnp.exp(c[tokens - 1:tokens, :] - c)
     row_scale = scaling * jnp.exp(c)
 
+    loads[1].wait()
+    loads[2].wait()
     for h in in_order:
         kd = (k_ref[:, at(h)].astype(F32) * tail[:, h:h + 1]).astype(BF16)
         kd_ref[:, at(h)] = kd
-        yb[h % own, h // own] = dot(kd, v_ref[:, at(h)], (0, 0))
+        put(yb, h, dot(kd, v_ref[:, at(h)], (0, 0)))
+    for load in loads[3:]:
+        load.wait()
     pl.semaphore_wait(barrier, SIDE + depth + group - 3)
 
     totals = over_y(tb, trb, 0)
@@ -145,7 +167,7 @@
     wholes = over_z(tz, tzr, 0, True)
 
     def own_decay(part, unit):
-        return jnp.exp(trb[part, unit:unit + 1])
+        return jnp.exp(trb[part, unit // CUT:unit // CUT + 1])
 
     for h in in_order:
         gaps = c[:, h:h + 1] - c_rows[h:h + 1, :]
@@ -169,28 +191,30 @@
         state = jnp.zeros((span, size), F32)
         for part in range(depth):
             zo[unit, part] = state
-            state = jnp.exp(tzr[part, unit:unit + 1]) * state + zrb[unit, part]
-        moving.append(over_z(zo.at[unit], zi.at[unit], 1 + own + unit))
+            state = jnp.exp(tzr[part, unit // CUT:unit // CUT + 1]) * state + zrb[unit, part]
+        moving.append(over_z(zo.at[unit], zi.at[unit], 1 + len(units) + unit))
     for h in in_order:
         qd_ref[:, at(h)] = (q_ref[:, at(h)].astype(F32) * row_scale[:, h:h + 1]).astype(BF16)
         u_ref[:, at(h)] = cot_ref[:, at(h)].astype(F32) * gain_ref[:, at(h)]
     out = []
     for unit in units:
         moving[unit].finish()
-        state = zi[unit].reshape(size, size)
+        state = zi[unit].reshape(rows, size)
         for part in range(SIDE):
             yo[unit, part] = state
             if part < SIDE - 1:
                 state = own_decay(part, unit) * state + yrb[unit, part]
-        out.append(over_y(yo.at[unit], yi.at[unit], 1 + own + unit))
+        out.append(over_y(yo.at[unit], yi.at[unit], 1 + len(units) + unit))
 
     squares = jnp.zeros((tokens, size), F32)
     slopes = jnp.zeros((tokens, size), F32)
-    for unit in units:
-        out[unit].finish()
+    for place in range(own):
+        pieces = range(place * CUT, (place + 1) * CUT)
+        for unit in pieces:
+            out[unit].finish()
         for part in range(SIDE):
-            h = part * own + unit
-            state = yi[unit, part].astype(BF16)
+            h = part * own + place
+            state = jnp.concatenate([yi[unit, part] for unit in pieces], axis=0).astype(BF16)
             s_ref[h] = state
             o = o_ref[:, at(h)] + dot(qd_ref[:, at(h)], state, (1, 0))
             o_ref[:, at(h)] = o
@@ -207,15 +231,16 @@
     inverse = jnp.transpose(jnp.broadcast_to(inverse_row, (size, tokens)))
     pull = jnp.transpose(jnp.broadcast_to(pull_row, (size, tokens)))
 
-    first = 1 + 2 * own
+    first = 1 + 2 * len(units)
     moving = []
-    for unit in units:
+    for place in range(own):
         for part in range(SIDE):
-            h = part * own + unit
+            h = part * own + place
             do = (inverse * u_ref[:, at(h)] - o_ref[:, at(h)] * pull).astype(BF16)
             do_ref[:, at(h)] = do
-            yb2[unit, part] = dot(qd_ref[:, at(h)], do, (0, 0))
-        moving.append(over_y(yb2.at[unit], yrb2.at[unit], first + unit))
+            put(yb2, h, dot(qd_ref[:, at(h)], do, (0, 0)))
+        for unit in range(place * CUT, (place + 1) * CUT):
+            moving.append(over_y(yb2.at[unit], yrb2.at[unit], first + unit))
     for h in in_order:
         ds_ref[h] = (dot(do_ref[:, at(h)], v_ref[:, at(h)], (1, 1)) * w_ref[h]).astype(BF16)
     out = []
@@ -238,25 +263,27 @@
         state = jnp.zeros((span, size), F32)
         for part in reversed(range(depth)):
             zo2[unit, part] = state
-            state = jnp.exp(tzr[part, unit:unit + 1]) * state + zrb2[unit, part]
-        moving.append(over_z(zo2.at[unit], zi2.at[unit], first + own + unit))
+            state = jnp.exp(tzr[part, unit // CUT:unit // CUT + 1]) * state + zrb2[unit, part]
+        moving.append(over_z(zo2.at[unit], zi2.at[unit], first + len(units) + unit))
     for h in in_order:
         gkl_ref[:, at(h)] = dot(ds_ref[h], q_ref[:, at(h)], (0, 0))
         gvl_ref[:, at(h)] = dot(sc_ref[h], do_ref[:, at(h)], (0, 0))
     out = []
     for unit in units:
         moving[unit].finish()
-        state = zi2[unit].reshape(size, size)
+        state = zi2[unit].reshape(rows, size)
         for part in reversed(range(SIDE)):
             yo2[unit, part] = state
             if part > 0:
                 state = own_decay(part, unit) * state + yrb2[unit, part]
-        out.append(over_y(yo2.at[unit], yi2.at[unit], first + own + unit))
-    for unit in units:
-        out[unit].finish()
+        out.append(over_y(yo2.at[unit], yi2.at[unit], first + len(units) + unit))
+    for place in range(own):
+        pieces = range(place * CUT, (place + 1) * CUT)
+        for unit in pieces:
+            out[unit].finish()
         for part in range(SIDE):
-            h = part * own + unit
-            state = yi2[unit, part].astype(BF16)
+            h = part * own + place
+            state = jnp.concatenate([yi2[unit, part] for unit in pieces], axis=0).astype(BF16)
             gk_ref[:, at(h)] = (
                 gkl_ref[:, at(h)] + dot(v_ref[:, at(h)], state, (1, 1)) * tail[:, h:h + 1]
             ).astype(BF16)
@@ -265,6 +292,11 @@
             ).astype(BF16)
     for made in exchanges:
         made.drain()
+
+
+def hand_on(*refs):
+    for source, target in zip(refs[:4], refs[4:]):
+        target[...] = source[...]
 
 
 def per_device(queries, keys, values, log_decay, gain, cotangent):
@@ -279,15 +311,17 @@
     flat = (tokens, width)
     V = pltpu.VMEM
     Sem = pltpu.SemaphoreType.DMA
-    y_slots = V((own, SIDE, size, size), F32)
-    z_slots = V((own, depth, size // depth, size), F32)
+    count = own * CUT
+    rows = size // CUT
+    y_slots = V((count, SIDE, rows, size), F32)
+    z_slots = V((count, depth, rows // depth, size), F32)
     way = [y_slots, y_slots, z_slots, z_slots, z_slots, z_slots, y_slots, y_slots]
-    steps = 1 + 4 * own
+    steps = 1 + 4 * count
     out = jax.ShapeDtypeStruct(flat, BF16)
-    return pl.pallas_call(
+    results = pl.pallas_call(
         functools.partial(kernel, seq_count, group, float(width * group)),
         out_shape=(out, out, out, out),
-        in_specs=[block] * 6,
+        in_specs=[pl.BlockSpec(memory_space=pl.ANY)] * 6,
         out_specs=(block,) * 4,
         scratch_shapes=[
             V(square, F32), V(square, BF16), V(square, BF16),
@@ -301,10 +335,21 @@
             Sem((steps, SIDE)), Sem((steps, SIDE)),
             Sem((steps, depth)), Sem((steps, depth)),
             Sem((1, group)), Sem((1, group)),
+            V(flat, BF16), V(flat, BF16), V(flat, BF16),
+            V((heads, tokens), F32), V((1, width), F32), V(flat, BF16), Sem((6,)),
         ],
         compiler_params=pltpu.CompilerParams(collective_id=0, has_side_effects=True),
         name="attention_both_ways",
     )(queries, keys, values, log_decay.T, gain.reshape(1, width), cotangent)
+    tile = pl.BlockSpec((tokens // 1, width), lambda i: (i, 0))
+    return pl.pallas_call(
+        hand_on,
+        grid=(1,),
+        out_shape=(out, out, out, out),
+        in_specs=[tile] * 4,
+        out_specs=(tile,) * 4,
+        name="hand_on",
+    )(*results)
 
 
 def solution(mesh):

time: 86.6 us -> 83.2 us (0.961)
  the two profiles are of different devices: /device:TPU:32 before, /device:TPU:8 now
where the time goes in v4:
time: 83.2 us; the launch traced here: 83.1 us
  Pallas kernels  82.4 us (99%)
    pallas_call x1, Pallas kernels, per_device(): pl.pallas_call(functools.partial(kernel, seq_count, group, float(width *...  80.2 us
    pallas_call x1, Pallas kernels, per_device(): pl.pallas_call(hand_on, grid=(1,), out_shape=(out, out, out, out), in_spe...  2.17 us

profile of v4, /device:TPU:8, one launch (start us, length us, event | category | flops | bytes accessed | tf_op | source)
XLA Modules:
  0.0 83.1 jit_solution(15108109552269746191)
XLA Ops:
  0.6 80.2 %attention_both_ways.1 = (bf16[128,1024]{1,0:T(8,128)(2,1)}, bf16[128,1024]{1,0:T(8,128)(2,1)}, bf16[128,1024]{1,0:T(8,128)(2,1)}, bf16[128,1024]{1,0:T(8,128)(2,1)}) custom-call(bf16[128,1024]{1,0:T(8,128)(2,1)} %q_in.1, bf16[128,1024]{1,0:T(8,128)(2,1)} %k_in.1, bf16[128,1024]{1,0:T(8,128)(2,1)} %v_in.1, f32[8,128]{1,0:T(8,128)} %bitcast.2, ...), custom_call_target="tpu_custom_call" | custom-call | tf_op jit(solution)/shard_map/attention_both_ways/pallas_call | solution.py:321
  80.9 2.2 %hand_on.1 = (bf16[128,1024]{1,0:T(8,128)(2,1)}, bf16[128,1024]{1,0:T(8,128)(2,1)}, bf16[128,1024]{1,0:T(8,128)(2,1)}, bf16[128,1024]{1,0:T(8,128)(2,1)}) custom-call(bf16[128,1024]{1,0:T(8,128)(2,1)} %get-tuple-element.8.refs_0_, bf16[128,1024]{1,0:T(8,128)(2,1)} %get-tuple-element.9.refs_1_, bf16[128,1024]{1,0:T(8,128)(2,1)} %get-tuple-element.10.refs_2_, ...), custom_call_target="tpu_custom_call" | custom-call | tf_op jit(solution)/shard_map/hand_on/pallas_call | solution.py:345

commit v5 on v4

--- a/solution.py
+++ b/solution.py
@@ -170,10 +170,8 @@
         return jnp.exp(trb[part, unit // CUT:unit // CUT + 1])
 
     for h in in_order:
-        gaps = c[:, h:h + 1] - c_rows[h:h + 1, :]
-        weights = jnp.where(causal, jnp.exp(jnp.where(causal, gaps, 0.0)), 0.0) * scaling
-        w_ref[h] = weights
-        sc_ref[h] = (dot(q_ref[:, at(h)], k_ref[:, at(h)], (1, 1)) * weights).astype(BF16)
+        qd_ref[:, at(h)] = (q_ref[:, at(h)].astype(F32) * row_scale[:, h:h + 1]).astype(BF16)
+        u_ref[:, at(h)] = cot_ref[:, at(h)].astype(F32) * gain_ref[:, at(h)]
     out = []
     for unit in units:
         moving[unit].finish()
@@ -183,7 +181,10 @@
         zb[unit] = state.reshape(depth, span, size)
         out.append(over_z(zb.at[unit], zrb.at[unit], 1 + unit))
     for h in in_order:
-        o_ref[:, at(h)] = dot(sc_ref[h], v_ref[:, at(h)], (1, 0))
+        gaps = c[:, h:h + 1] - c_rows[h:h + 1, :]
+        weights = jnp.where(causal, jnp.exp(jnp.where(causal, gaps, 0.0)), 0.0) * scaling
+        w_ref[h] = weights
+        sc_ref[h] = (dot(q_ref[:, at(h)], k_ref[:, at(h)], (1, 1)) * weights).astype(BF16)
     wholes.finish()
     moving = []
     for unit in units:
@@ -194,8 +195,7 @@
             state = jnp.exp(tzr[part, unit // CUT:unit // CUT + 1]) * state + zrb[unit, part]
         moving.append(over_z(zo.at[unit], zi.at[unit], 1 + len(units) + unit))
     for h in in_order:
-        qd_ref[:, at(h)] = (q_ref[:, at(h)].astype(F32) * row_scale[:, h:h + 1]).astype(BF16)
-        u_ref[:, at(h)] = cot_ref[:, at(h)].astype(F32) * gain_ref[:, at(h)]
+        o_ref[:, at(h)] = dot(sc_ref[h], v_ref[:, at(h)], (1, 0))
     out = []
     for unit in units:
         moving[unit].finish()
@@ -242,7 +242,7 @@
         for unit in range(place * CUT, (place + 1) * CUT):
             moving.append(over_y(yb2.at[unit], yrb2.at[unit], first + unit))
     for h in in_order:
-        ds_ref[h] = (dot(do_ref[:, at(h)], v_ref[:, at(h)], (1, 1)) * w_ref[h]).astype(BF16)
+        normed_ref[:, at(h)] = (o_ref[:, at(h)] * inverse * gain_ref[:, at(h)]).astype(BF16)
     out = []
     for unit in units:
         moving[unit].finish()
@@ -252,7 +252,8 @@
         zb2[unit] = state.reshape(depth, span, size)
         out.append(over_z(zb2.at[unit], zrb2.at[unit], first + unit))
     for h in in_order:
-        normed_ref[:, at(h)] = (o_ref[:, at(h)] * inverse * gain_ref[:, at(h)]).astype(BF16)
+        ds_ref[h] = (dot(do_ref[:, at(h)], v_ref[:, at(h)], (1, 1)) * w_ref[h]).astype(BF16)
+    for h in in_order:
         gq_ref[:, at(h)] = (
             dot(ds_ref[h], k_ref[:, at(h)], (1, 0))
             + dot(do_ref[:, at(h)], s_ref[h], (1, 1)) * row_scale[:, h:h + 1]

time: 83.2 us -> 83 us (level)
  no operation moved by 1% of the time
where the time goes in v5:
time: 83 us; the launch traced here: 82.9 us
  Pallas kernels  82.2 us (99%)
    pallas_call x1, Pallas kernels, per_device(): pl.pallas_call(functools.partial(kernel, seq_count, group, float(width *...  80.1 us
    pallas_call x1, Pallas kernels, per_device(): pl.pallas_call(hand_on, grid=(1,), out_shape=(out, out, out, out), in_spe...  2.17 us

profile of v5, /device:TPU:8, one launch (start us, length us, event | category | flops | bytes accessed | tf_op | source)
XLA Modules:
  0.0 82.9 jit_solution(18082961036346372747)
XLA Ops:
  0.6 80.1 %attention_both_ways.1 = (bf16[128,1024]{1,0:T(8,128)(2,1)}, bf16[128,1024]{1,0:T(8,128)(2,1)}, bf16[128,1024]{1,0:T(8,128)(2,1)}, bf16[128,1024]{1,0:T(8,128)(2,1)}) custom-call(bf16[128,1024]{1,0:T(8,128)(2,1)} %q_in.1, bf16[128,1024]{1,0:T(8,128)(2,1)} %k_in.1, bf16[128,1024]{1,0:T(8,128)(2,1)} %v_in.1, f32[8,128]{1,0:T(8,128)} %bitcast.2, ...), custom_call_target="tpu_custom_call" | custom-call | tf_op jit(solution)/shard_map/attention_both_ways/pallas_call | solution.py:322
  80.7 2.2 %hand_on.1 = (bf16[128,1024]{1,0:T(8,128)(2,1)}, bf16[128,1024]{1,0:T(8,128)(2,1)}, bf16[128,1024]{1,0:T(8,128)(2,1)}, bf16[128,1024]{1,0:T(8,128)(2,1)}) custom-call(bf16[128,1024]{1,0:T(8,128)(2,1)} %get-tuple-element.8.refs_0_, bf16[128,1024]{1,0:T(8,128)(2,1)} %get-tuple-element.9.refs_1_, bf16[128,1024]{1,0:T(8,128)(2,1)} %get-tuple-element.10.refs_2_, ...), custom_call_target="tpu_custom_call" | custom-call | tf_op jit(solution)/shard_map/hand_on/pallas_call | solution.py:346
